TPU v7x, 32 devices: a whole 2x2x4 slice. The times are simulated.
32 devices in a mesh: row: 8 (over y, x, core), col: 4 (over z).
Axes of the slice: x: 2, y: 2, z: 4, core: 2. Of those that a mesh axis runs over, the one named last changes fastest.
Arguments:
- right_sides: float32 [64, 32768], P(None, ('row', 'col'))
- diag_tiles: float32 [32, 1024, 1024], P(('row', 'col')), as said below
- low_rank: float32 [32, 4, 8, 2, 12, 1024], P('row', 'col'), as said below
- tile_ranks: int32 [32, 4, 8], P('row', 'col'), may hold values from 1 to 12, as said below
- inv_factor: float32 [256, 8, 128, 128], P(('row', 'col')), as said below
- sub_sizes: int32 [64], replicated, may hold values from 1 to 8, 256 in all
Outputs:
- solution: float32 [64, 32768], P(None, ('row', 'col'))
- residual: float32 [64, 32768], P(None, ('row', 'col'))
Inputs may be any that keep to these rules, and one draw needn't show every extreme that they name: `low_rank`: tile (j, i) holds the two factors of tile (i, j) in swapped order, and a diagonal tile's two factors are equal, so S is symmetric. `tile_ranks`: the rank of tile (i, j) equals that of tile (j, i); diagonal tiles have rank 12. `diag_tiles`: each tile is symmetric positive definite. `inv_factor`: the block at distance 0 of every span is lower triangular with a positive diagonal. `sub_sizes`: the sizes sum to 256.
All inputs are finite; a program needn't handle non-finite values.
Results may differ from a plain program's by a relative error of at most 0.0003.
Values sent between devices are 32-bit elements; how exact they have to be, the bound alone decides.
A program may use at most 128 MiB of HBM per device.

v0:
```python
import jax
import jax.numpy as jnp
from jax import lax
from jax.sharding import PartitionSpec as P

RANK = 12
finest = lax.Precision.HIGHEST


def shifted(x, axis, by):
    size = lax.axis_size(axis)
    pairs = [(i, i + by) for i in range(size) if 0 <= i + by < size]
    return lax.ppermute(x, axis, pairs)


def span_weights(sub_sizes, per_device, reach_len):
    span_ids = lax.axis_index(("row", "col")) * per_device + lax.iota(jnp.int32, per_device)
    ending = jnp.cumsum(sub_sizes)
    opening = ending - sub_sizes
    inside = (span_ids[:, None] >= opening[None, :]) & (span_ids[:, None] < ending[None, :])
    position = span_ids - jnp.sum(jnp.where(inside, opening[None, :], 0), axis=1)
    return (lax.iota(jnp.int32, reach_len)[None, :] <= position[:, None]).astype(jnp.float32)


def precondition(vector, inv_factor, weights):
    rhs_count, tile_len = vector.shape
    per_device = inv_factor.shape[0]
    reach_len = inv_factor.shape[1]
    span_len = inv_factor.shape[2]
    before = shifted(vector, ("row", "col"), 1)
    joined = jnp.concatenate([before, vector], axis=1).reshape(rhs_count, 2 * per_device, span_len)
    windows = jnp.stack(
        [joined[:, per_device - behind : 2 * per_device - behind] for behind in range(reach_len)],
        axis=2,
    )
    windows = windows * weights[None, :, :, None]
    forward = jnp.einsum("ltji,klti->klj", inv_factor, windows, precision=finest)
    spread = (
        jnp.einsum("ltji,klj->klti", inv_factor, forward, precision=finest)
        * weights[None, :, :, None]
    )
    placed = jnp.zeros_like(joined)
    for behind in range(reach_len):
        placed = placed + jnp.pad(
            spread[:, :, behind], ((0, 0), (per_device - behind, behind), (0, 0))
        )
    returned = shifted(placed[:, :per_device].reshape(rhs_count, tile_len), ("row", "col"), -1)
    return placed[:, per_device:].reshape(rhs_count, tile_len) + returned


def operate(vector, diag_tiles, low_rank, tile_ranks):
    rhs_count, tile_len = vector.shape
    tile_rows = low_rank.shape[0]
    local_part = jnp.dot(vector, diag_tiles[0], precision=finest)
    left_factor = low_rank[:, 0, :, 0]
    right_factor = low_rank[:, 0, :, 1]
    weights = (lax.iota(jnp.int32, RANK)[None, None, :] < tile_ranks[:, 0, :, None]).astype(
        jnp.float32
    )
    initial = jnp.zeros((rhs_count, tile_rows * tile_len), jnp.float32)
    piece = lax.all_gather(vector, "row", axis=1, tiled=True)
    count_tiles = piece.shape[1] // tile_len
    pieces = piece.reshape(rhs_count, count_tiles, tile_len)
    coeffs = (
        jnp.einsum("bmqt,pmt->bmqp", right_factor, pieces, precision=finest)
        * weights[:, :, :, None]
    )
    added = jnp.einsum("bmqt,bmqp->pbt", left_factor, coeffs, precision=finest)
    partial_rows = initial + added.reshape(rhs_count, tile_rows * tile_len)
    summed = lax.psum_scatter(partial_rows, "col", scatter_dimension=1, tiled=True)
    return local_part + summed


def solve_spd(matrix, target):
    factor = jnp.linalg.cholesky(matrix)
    return jax.scipy.linalg.cho_solve((factor, True), target)


def gram_of(first_block, second_block):
    return jnp.dot(first_block, second_block.T, precision=finest)


def apply_coeffs(coeffs, block_rows):
    return jnp.dot(coeffs.T, block_rows, precision=finest)


def global_sum(terms):
    return lax.psum((terms[0], terms[1]), ("row", "col"))


def body(right_sides, diag_tiles, low_rank, tile_ranks, inv_factor, sub_sizes):
    weights = span_weights(sub_sizes, inv_factor.shape[0], inv_factor.shape[1])
    residual = right_sides
    search = precondition(residual, inv_factor, weights)
    images = operate(search, diag_tiles, low_rank, tile_ranks)
    rho_now, curvature = global_sum((gram_of(search, residual), gram_of(search, images)))
    step_size = solve_spd(curvature, rho_now)
    solution = apply_coeffs(step_size, search)
    residual = residual - apply_coeffs(step_size, images)
    precond = precondition(residual, inv_factor, weights)
    product = operate(precond, diag_tiles, low_rank, tile_ranks)
    rho_next, self_term, cross_term = lax.psum(
        (gram_of(precond, residual), gram_of(precond, product), gram_of(search, product)),
        ("row", "col"),
    )
    beta_mix = solve_spd(rho_now, rho_next)
    curvature = (
        self_term
        + jnp.dot(cross_term.T, beta_mix, precision=finest)
        + jnp.dot(beta_mix.T, cross_term, precision=finest)
        + jnp.dot(beta_mix.T, jnp.dot(curvature, beta_mix, precision=finest), precision=finest)
    )
    search = precond + apply_coeffs(beta_mix, search)
    images = product + apply_coeffs(beta_mix, images)
    step_size = solve_spd(curvature, rho_next)
    solution = solution + apply_coeffs(step_size, search)
    residual = residual - apply_coeffs(step_size, images)
    return (solution, residual)


def solution(mesh):
    placed = (
        P(None, ("row", "col")),
        P(("row", "col"), None, None),
        P("row", "col", None, None, None, None),
        P("row", "col", None),
        P(("row", "col"), None, None, None),
        P(),
    )
    return jax.shard_map(
        body,
        mesh=mesh,
        in_specs=placed,
        out_specs=(P(None, ("row", "col")), P(None, ("row", "col"))),
        check_vma=False,
    )
```

profile of v0, /device:TPU:0, one launch (start us, length us, event | category | flops | bytes accessed | tf_op | source)
XLA Modules:
  0.0 335.0 jit_solution(9789738542311892284)
XLA Ops:
  7.2 5.0 %collective-permute-start = (f32[64,1024]{1,0:T(8,128)}, f32[64,1024]{1,0:T(8,128)S(1)}, u32[]{:S(2)}, u32[]{:S(2)}) collective-permute-start(f32[64,1024]{1,0:T(8,128)} %param.9), channel_id=1, source_target_pairs={{0,1},{1,2},{2,3},{3,4},{4,5},{5,6},{6,7},{7,8},{8,9},{9,10},{10,1... | collective-permute-start | bytes 786440 | tf_op jit(solution)/shard_map/ppermute | solution.py:13
  14.1 3.9 %collective-permute-done = f32[64,1024]{1,0:T(8,128)S(1)} collective-permute-done((f32[64,1024]{1,0:T(8,128)}, f32[64,1024]{1,0:T(8,128)S(1)}, u32[]{:S(2)}, u32[]{:S(2)}) %collective-permute-start) | collective-permute-done | bytes 262176 | tf_op jit(solution)/shard_map/ppermute | solution.py:13
  19.7 1.8 copy-done
  21.5 4.6 %fusion.20 = f32[64,8,128,1]{2,0,3,1:T(8,128)S(1)} fusion(f32[8,8,128,128]{3,2,1,0:T(8,128)S(1)} %copy-done, f32[64,8,8,128]{3,0,2,1:T(8,128)S(1)} %fusion.62, f32[8,8]{1,0:T(8,128)S(1)} %fusion.89), kind=kOutput, calls=%fused_computation.23 | convolution fusion | flops 805830656 | bytes 6553856 | tf_op jit(solution)/shard_map/ltji,klti->klj/dot_general | solution.py:37
  26.1 2.4 multiply_bitcast_fusion.1
  30.3 8.7 %collective-permute-done.1 = f32[64,1024]{1,0:T(8,128)S(1)} collective-permute-done((f32[64,1024]{1,0:T(8,128)S(1)}, f32[64,1024]{1,0:T(8,128)S(1)}, u32[]{:S(2)}, u32[]{:S(2)}) %collective-permute-start.1) | collective-permute-done | bytes 262176 | tf_op jit(solution)/shard_map/ppermute | solution.py:13
  40.5 6.1 %fusion.91 = (f32[4,1,8,1,12,1024]{5,3,4,2,1,0:T(1,128)S(1)}, f32[4,1,8,1,12,1024]{5,3,4,2,1,0:T(1,128)S(1)}) fusion(f32[4,1,8,2,12,1024]{5,3,4,2,1,0:T(2,128)} %param.11), kind=kLoop, calls=%fused_computation.139 | loop fusion | bytes 6291456 | tf_op jit(solution)/shard_map/slice | solution.py:55
  46.6 25.1 %all-gather.3.cloned.1.call-done = f32[64,8192]{1,0:T(8,128)} async-done(((f32[64,1024]{1,0:T(8,128)}), f32[64,8192]{1,0:T(8,128)}) %all-gather.3.cloned.1.call-update) | async-done | bytes 2097168 | tf_op jit(solution)/shard_map/all_gather | solution.py:61
  71.7 2.8 copy.231
  74.5 3.6 %fusion.37 = f32[4,8,12,64]{3,2,0,1:T(8,128)S(1)} fusion(f32[4,1,8,1,12,1024]{5,3,4,2,1,0:T(1,128)S(1)} %get-tuple-element.10, f32[64,8,1024,1]{2,1,0,3:T(8,128)S(1)} %bitcast.313, f32[4,8,12]{2,0,1:T(4,128)S(1)} %fusion.88), kind=kOutput, calls=%fused_computation.33 | convolution fusion | flops 302014464 | bytes 3769856 | tf_op jit(solution)/shard_map/bmqt,pmt->bmqp/dot_general | solution.py:65
  78.1 1.6 fusion.18
  82.3 25.9 %reduce-scatter.3.cloned.1.call-done = f32[64,1024]{1,0:T(8,128)} async-done(((f32[64,4096]{1,0:T(8,128)}), f32[64,1024]{1,0:T(8,128)}) %reduce-scatter.3.cloned.1.call-update) | async-done | bytes 262160 | tf_op jit(solution)/shard_map/reduce_scatter | solution.py:70
  108.2 4.9 %fusion.26 = f32[64,1024]{1,0:T(8,128)S(1)} fusion(f32[64,1024]{1,0:T(8,128)} %reduce-scatter.3.cloned.1.call-done, f32[64,1024]{1,0:T(8,128)S(1)} %copy-done.2, f32[1,1024,1024]{2,1,0:T(8,128)} %param.10), kind=kOutput, calls=%fused_computation.25 | convolution fusion | flops 805371904 | bytes 4980736 | tf_op jit(solution)/shard_map/dot_general | solution.py:54
  114.1 39.2 %all-reduce.17 = (f32[64,64]{0,1:T(8,128)S(1)}, f32[64,64]{0,1:T(8,128)S(1)}) all-reduce(f32[64,64]{0,1:T(8,128)S(1)} %fusion.95, f32[64,64]{0,1:T(8,128)S(1)} %fusion.94), channel_id=1, replica_groups=mesh['row'=8,'col'=4] {'row','col'}, use_global_device_ids=true, to_apply=%region_6.8 | all-reduce | flops 8192 | bytes 65536 | tf_op jit(solution)/shard_map/psum | solution.py:88
  153.4 5.8 %cholesky.59 = f32[64,64]{1,0:T(8,128)S(1)} custom-call(f32[64,64]{1,0:T(8,128)S(1)} %fusion.87), custom_call_target="Cholesky" | custom-call | tf_op jit(solution)/shard_map/jit(cholesky)/cholesky | solution.py:75
  161.4 5.7 %custom-call.9 = f32[1,64,64]{1,2,0:T(8,128)S(1)} custom-call(f32[1,64,64]{2,1,0:T(8,128)} %fusion.70), custom_call_target="InvertDiagBlocksLowerTriangular" | custom-call | tf_op jit(solution)/shard_map/jit(_cho_solve)/triangular_solve | solution.py:76
  168.9 3.8 %collective-permute-start.2 = (f32[64,1024]{1,0:T(8,128)S(1)}, f32[64,1024]{1,0:T(8,128)S(1)}, u32[]{:S(2)}, u32[]{:S(2)}) collective-permute-start(f32[64,1024]{1,0:T(8,128)S(1)} %convolution_subtract_fusion.1), channel_id=1, source_target_pairs={{0,1},{1,2},{2,3},{3,4},{4,5},{5,6},{6,7},{7,8},{8,9},{9,10},{10,1... | collective-permute-start | bytes 786440 | tf_op jit(solution)/shard_map/ppermute | solution.py:13
  172.7 4.7 %collective-permute-done.2 = f32[64,1024]{1,0:T(8,128)S(1)} collective-permute-done((f32[64,1024]{1,0:T(8,128)S(1)}, f32[64,1024]{1,0:T(8,128)S(1)}, u32[]{:S(2)}, u32[]{:S(2)}) %collective-permute-start.2) | collective-permute-done | bytes 262176 | tf_op jit(solution)/shard_map/ppermute | solution.py:13
  178.2 1.7 copy-done.1
  179.9 4.6 %fusion.23 = f32[64,8,128,1]{2,0,3,1:T(8,128)S(1)} fusion(f32[8,8,128,128]{3,2,1,0:T(8,128)S(1)} %copy-done.1, f32[64,8,8,128]{3,0,2,1:T(8,128)S(1)} %fusion.54, f32[8,8]{1,0:T(8,128)S(1)} %copy-done.9), kind=kOutput, calls=%fused_computation.24 | convolution fusion | flops 805830656 | bytes 6553856 | tf_op jit(solution)/shard_map/ltji,klti->klj/dot_general | solution.py:37
  184.6 2.4 multiply_bitcast_fusion
  188.7 9.1 %collective-permute-done.3 = f32[64,1024]{1,0:T(8,128)S(1)} collective-permute-done((f32[64,1024]{1,0:T(8,128)S(1)}, f32[64,1024]{1,0:T(8,128)S(1)}, u32[]{:S(2)}, u32[]{:S(2)}) %collective-permute-start.3) | collective-permute-done | bytes 262176 | tf_op jit(solution)/shard_map/ppermute | solution.py:13
  198.8 29.4 %all-gather.5.cloned.1.call-done = f32[64,8192]{1,0:T(8,128)} async-done(((f32[64,1024]{1,0:T(8,128)}), f32[64,8192]{1,0:T(8,128)}) %all-gather.5.cloned.1.call-update) | async-done | bytes 2097168 | tf_op jit(solution)/shard_map/all_gather | solution.py:61
  228.3 2.8 copy.233
  231.0 3.6 %fusion.47 = f32[4,8,12,64]{3,2,0,1:T(8,128)S(1)} fusion(f32[4,1,8,1,12,1024]{5,3,4,2,1,0:T(1,128)S(1)} %get-tuple-element.10, f32[64,8,1024,1]{2,1,0,3:T(8,128)S(1)} %bitcast.312, f32[4,8,12]{2,0,1:T(4,128)S(1)} %fusion.88), kind=kOutput, calls=%fused_computation.35 | convolution fusion | flops 302014464 | bytes 3769856 | tf_op jit(solution)/shard_map/bmqt,pmt->bmqp/dot_general | solution.py:65
  237.4 5.8 %cholesky.70 = f32[64,64]{1,0:T(8,128)S(1)} custom-call(f32[64,64]{1,0:T(8,128)S(1)} %fusion.82), custom_call_target="Cholesky" | custom-call | tf_op jit(solution)/shard_map/jit(cholesky)/cholesky | solution.py:75
  244.6 4.9 %custom-call.10 = f32[1,64,64]{1,2,0:T(8,128)S(1)} custom-call(f32[1,64,64]{2,1,0:T(8,128)S(1)} %fusion.71), custom_call_target="InvertDiagBlocksLowerTriangular" | custom-call | tf_op jit(solution)/shard_map/jit(_cho_solve)/triangular_solve | solution.py:76
  249.9 15.0 %reduce-scatter.5.cloned.1.call-done = f32[64,1024]{1,0:T(8,128)} async-done(((f32[64,4096]{1,0:T(8,128)}), f32[64,1024]{1,0:T(8,128)}) %reduce-scatter.5.cloned.1.call-update) | async-done | bytes 262160 | tf_op jit(solution)/shard_map/reduce_scatter | solution.py:70
  264.8 4.8 %fusion.29 = f32[64,1024]{1,0:T(8,128)S(1)} fusion(f32[64,1024]{1,0:T(8,128)} %reduce-scatter.5.cloned.1.call-done, f32[64,1024]{1,0:T(8,128)S(1)} %copy-done.3, f32[1,1024,1024]{2,1,0:T(8,128)} %param.10), kind=kOutput, calls=%fused_computation.26 | convolution fusion | flops 805371904 | bytes 4980736 | tf_op jit(solution)/shard_map/dot_general | solution.py:54
  270.4 40.1 %all-reduce.16 = (f32[64,64]{1,0:T(8,128)S(1)}, f32[64,64]{1,0:T(8,128)S(1)}, f32[64,64]{0,1:T(8,128)S(1)}) all-reduce(f32[64,64]{1,0:T(8,128)S(1)} %fusion.98, f32[64,64]{1,0:T(8,128)S(1)} %fusion.97, f32[64,64]{0,1:T(8,128)S(1)} %fusion.96), channel_id=1, replica_groups=mesh['row'=8,'col'=4] {'row','col'}, use_global_device_ids=true, to_apply=%region_10.13 | all-reduce | flops 12288 | bytes 98304 | tf_op jit(solution)/shard_map/psum | solution.py:102
  312.8 5.8 %cholesky.81 = f32[64,64]{1,0:T(8,128)S(1)} custom-call(f32[64,64]{1,0:T(8,128)S(1)} %fusion.77), custom_call_target="Cholesky" | custom-call | tf_op jit(solution)/shard_map/jit(cholesky)/cholesky | solution.py:75
  320.0 4.9 %custom-call.11 = f32[1,64,64]{1,2,0:T(8,128)S(1)} custom-call(f32[1,64,64]{2,1,0:T(8,128)S(1)} %fusion.72), custom_call_target="InvertDiagBlocksLowerTriangular" | custom-call | tf_op jit(solution)/shard_map/jit(_cho_solve)/triangular_solve | solution.py:76
  (111 shorter events, 29.6 us)
Async XLA Ops:
  7.2 64.6 %all-gather.3.cloned.1.call-start = ((), (), s32[]{:S(2)}) async-start(), calls=%async_computation.2 | async-start | bytes 2359296 | tf_op jit(solution)/shard_map/all_gather | solution.py:61
  7.2 10.8 %collective-permute-start = (f32[64,1024]{1,0:T(8,128)}, f32[64,1024]{1,0:T(8,128)S(1)}, u32[]{:S(2)}, u32[]{:S(2)}) collective-permute-start(f32[64,1024]{1,0:T(8,128)} %param.9), channel_id=1, source_target_pairs={{0,1},{1,2},{2,3},{3,4},{4,5},{5,6},{6,7},{7,8},{8,9},{9,10},{10,1... | collective-permute-start | bytes 786440 | tf_op jit(solution)/shard_map/ppermute | solution.py:13
  14.1 12.0 %copy-start.8 = (f32[8,8]{1,0:T(8,128)}, f32[8,8]{1,0:T(8,128)S(1)}, u32[]{:S(2)}) copy-start(f32[8,8]{1,0:T(8,128)S(1)} %fusion.89) | copy-start | bytes 772
  19.3 2.2 copy-start
  28.7 11.6 %copy-start.10 = (s32[4,1,8]{2,1,0:T(1,128)S(1)}, s32[4,1,8]{2,1,0:T(1,128)}, u32[]{:S(2)}) copy-start(s32[4,1,8]{2,1,0:T(1,128)} %param.12) | copy-start | bytes 388
  29.0 10.0 %collective-permute-start.1 = (f32[64,1024]{1,0:T(8,128)S(1)}, f32[64,1024]{1,0:T(8,128)S(1)}, u32[]{:S(2)}, u32[]{:S(2)}) collective-permute-start(f32[64,1024]{1,0:T(8,128)S(1)} %bitcast.318), channel_id=1, source_target_pairs={{1,0},{2,1},{3,2},{4,3},{5,4},{6,5},{7,6},{8,7},{9,8},{10,9},{11,1... | collective-permute-start | bytes 786440 | tf_op jit(solution)/shard_map/ppermute | solution.py:13
  39.8 68.4 %reduce-scatter.3.cloned.1.call-start = ((), (), s32[]{:S(2)}) async-start(), calls=%async_computation.3 | async-start | bytes 1310720 | tf_op jit(solution)/shard_map/reduce_scatter | solution.py:70
  79.7 1.3 copy-start.2
  80.8 147.5 %all-gather.5.cloned.1.call-start = ((), (), s32[]{:S(2)}) async-start(), calls=%async_computation.4 | async-start | bytes 2359296 | tf_op jit(solution)/shard_map/all_gather | solution.py:61
  113.1 0.7 copy-start.4
  168.9 8.6 %copy-start.6 = (f32[64,1024]{1,0:T(8,128)}, f32[64,1024]{1,0:T(8,128)S(1)}, u32[]{:S(2)}) copy-start(f32[64,1024]{1,0:T(8,128)S(1)} %convolution_subtract_fusion.1) | copy-start | bytes 786436
  168.9 8.6 %collective-permute-start.2 = (f32[64,1024]{1,0:T(8,128)S(1)}, f32[64,1024]{1,0:T(8,128)S(1)}, u32[]{:S(2)}, u32[]{:S(2)}) collective-permute-start(f32[64,1024]{1,0:T(8,128)S(1)} %convolution_subtract_fusion.1), channel_id=1, source_target_pairs={{0,1},{1,2},{2,3},{3,4},{4,5},{5,6},{6,7},{7,8},{8,9},{9,10},{10,1... | collective-permute-start | bytes 786440 | tf_op jit(solution)/shard_map/ppermute | solution.py:13
  177.7 2.2 copy-start.1
  177.8 2.2 copy-start.9
  187.4 10.4 %collective-permute-start.3 = (f32[64,1024]{1,0:T(8,128)S(1)}, f32[64,1024]{1,0:T(8,128)S(1)}, u32[]{:S(2)}, u32[]{:S(2)}) collective-permute-start(f32[64,1024]{1,0:T(8,128)S(1)} %bitcast.319), channel_id=1, source_target_pairs={{1,0},{2,1},{3,2},{4,3},{5,4},{6,5},{7,6},{8,7},{9,8},{10,9},{11,1... | collective-permute-start | bytes 786440 | tf_op jit(solution)/shard_map/ppermute | solution.py:13
  198.6 66.3 %reduce-scatter.5.cloned.1.call-start = ((), (), s32[]{:S(2)}) async-start(), calls=%async_computation.5 | async-start | bytes 1310720 | tf_op jit(solution)/shard_map/reduce_scatter | solution.py:70
  236.2 13.3 %copy-start.3 = (f32[64,1024]{1,0:T(8,128)S(1)}, f32[64,1024]{1,0:T(8,128)}, u32[]{:S(2)}) copy-start(f32[64,1024]{1,0:T(8,128)} %bitcast_add_fusion) | copy-start | bytes 786436
  236.2 13.3 %copy-start.7 = (f32[64,1024]{1,0:T(8,128)S(1)}, f32[64,1024]{1,0:T(8,128)}, u32[]{:S(2)}) copy-start(f32[64,1024]{1,0:T(8,128)} %copy-done.6) | copy-start | bytes 786436
  249.9 61.0 %copy-start.5 = (f32[64,1024]{1,0:T(8,128)S(1)}, f32[64,1024]{1,0:T(8,128)}, u32[]{:S(2)}) copy-start(f32[64,1024]{1,0:T(8,128)} %copy-done.4) | copy-start | bytes 786436
Sparse Core Ops, SparseCore 0:
  39.9 31.7 all-gather.2
  80.9 27.2 reduce-scatter.2
  198.7 29.5 all-gather.4
  237.4 27.3 reduce-scatter.4
where the time goes:
time: 341 us; the launch traced here: 335 us
  waiting for transfers between devices  122 us (36%)
  blocking collectives  79.3 us (23%)
  matrix products  43.8 us (13%)
  other arithmetic  41.8 us (12%)
  local copies, waits for them, and re-layouts  20.9 us (6%)
  between operations  14.9 us (4%)
  starting transfers between devices  12.5 us (4%)
    all_gather x2, waiting for transfers between devices, operate(): piece = lax.all_gather(vector, 'row', axis=1, tiled=True)  54.5 us
    reduce_scatter x2, waiting for transfers between devices, operate(): lax.psum_scatter(partial_rows, 'col', scatter_dimension=1, tiled=True)  40.8 us
    psum x1, blocking collectives, body(): lax.psum((gram_of(precond, residual), gram_of(precond, product), gram_of(...  40.1 us
    psum x1, blocking collectives, global_sum(): return lax.psum((terms[0], terms[1]), ('row', 'col'))  39.2 us
    ppermute x4, waiting for transfers between devices, shifted(): return lax.ppermute(x, axis, pairs)  26.4 us
    another operation x9, other arithmetic, solve_spd(): factor = jnp.linalg.cholesky(matrix)  19.7 us
    another operation x6, other arithmetic, solve_spd(): return jax.scipy.linalg.cho_solve((factor, True), target)  18 us
    ppermute x4, starting transfers between devices, shifted(): return lax.ppermute(x, axis, pairs)  11.4 us
  transfers between devices with their start and end apart: 8, of which 8 were waited for; matrix products, arithmetic and copies ran while one was open for 7% of the time, Pallas kernels for 0%

commit v1 on v0

--- a/solution.py
+++ b/solution.py
@@ -5,6 +5,16 @@
 
 RANK = 12
 finest = lax.Precision.HIGHEST
+
+
+def around_the_ring(value, axis, dim):
+    devices = lax.axis_size(axis)
+    current, blocks = (value, [value])
+    for _ in range(devices - 1):
+        current = lax.ppermute(current, axis, [(i, (i + 1) % devices) for i in range(devices)])
+        blocks.insert(0, current)
+    merged = jnp.concatenate(blocks, axis=dim)
+    return jnp.roll(merged, (lax.axis_index(axis) + 1) * value.shape[dim], axis=dim)
 
 
 def shifted(x, axis, by):
@@ -58,7 +68,7 @@
         jnp.float32
     )
     initial = jnp.zeros((rhs_count, tile_rows * tile_len), jnp.float32)
-    piece = lax.all_gather(vector, "row", axis=1, tiled=True)
+    piece = around_the_ring(vector, "row", 1)
     count_tiles = piece.shape[1] // tile_len
     pieces = piece.reshape(rhs_count, count_tiles, tile_len)
     coeffs = (

time: 341 us -> 379 us (1.11)
  waiting for transfers between devices: 122 us -> 160 us
    ppermute x0 -> x14, waiting for transfers between devices: none -> 90.8 us  [around_the_ring(): lax.ppermute(current, axis, [(i, (i + 1) % devices) for i in range(device...]
    all_gather x2 -> x0, waiting for transfers between devices: 54.5 us -> none  [operate(): piece = lax.all_gather(vector, 'row', axis=1, tiled=True)]
    unnamed x42 -> x74, local copies, waits for them, and re-layouts: 10.7 us -> 11.7 us
  transfers between devices with their start and end apart: 8 -> 20, of which waited for: 8 -> 20; matrix products, arithmetic and copies ran while one was open for 7% -> 5% of each run, Pallas kernels for 0% -> 0%
where the time goes in v1:
time: 379 us; the launch traced here: 373 us
  waiting for transfers between devices  160 us (42%)
  blocking collectives  79.2 us (21%)
  matrix products  43.9 us (12%)
  other arithmetic  41 us (11%)
  local copies, waits for them, and re-layouts  19.2 us (5%)
  between operations  15.4 us (4%)
  starting transfers between devices  13.9 us (4%)
    ppermute x14, waiting for transfers between devices, around_the_ring(): lax.ppermute(current, axis, [(i, (i + 1) % devices) for i in range(device...  90.8 us
    reduce_scatter x2, waiting for transfers between devices, operate(): lax.psum_scatter(partial_rows, 'col', scatter_dimension=1, tiled=True)  42.7 us
    psum x1, blocking collectives, body(): lax.psum((gram_of(precond, residual), gram_of(precond, product), gram_of(...  40 us
    psum x1, blocking collectives, global_sum(): return lax.psum((terms[0], terms[1]), ('row', 'col'))  39.2 us
    ppermute x4, waiting for transfers between devices, shifted(): return lax.ppermute(x, axis, pairs)  26.4 us
    another operation x9, other arithmetic, solve_spd(): factor = jnp.linalg.cholesky(matrix)  19.6 us
    another operation x6, other arithmetic, solve_spd(): return jax.scipy.linalg.cho_solve((factor, True), target)  17.9 us
    unnamed x74, local copies, waits for them, and re-layouts  11.7 us
  transfers between devices with their start and end apart: 20, of which 20 were waited for; matrix products, arithmetic and copies ran while one was open for 5% of the time, Pallas kernels for 0%

profile of v1, /device:TPU:0, one launch (start us, length us, event | category | flops | bytes accessed | tf_op | source)
XLA Modules:
  0.0 372.5 jit_solution(655319926039814902)
XLA Ops:
  7.2 5.0 %collective-permute-start = (f32[64,1024]{1,0:T(8,128)}, f32[64,1024]{1,0:T(8,128)S(1)}, u32[]{:S(2)}, u32[]{:S(2)}) collective-permute-start(f32[64,1024]{1,0:T(8,128)} %param.11), channel_id=1, source_target_pairs={{0,1},{1,2},{2,3},{3,4},{4,5},{5,6},{6,7},{7,8},{8,9},{9,10},{10,1... | collective-permute-start | bytes 786440 | tf_op jit(solution)/shard_map/ppermute | solution.py:23
  14.1 3.9 %collective-permute-done = f32[64,1024]{1,0:T(8,128)S(1)} collective-permute-done((f32[64,1024]{1,0:T(8,128)}, f32[64,1024]{1,0:T(8,128)S(1)}, u32[]{:S(2)}, u32[]{:S(2)}) %collective-permute-start) | collective-permute-done | bytes 262176 | tf_op jit(solution)/shard_map/ppermute | solution.py:23
  21.5 4.6 %fusion.22 = f32[64,8,128,1]{2,0,3,1:T(8,128)S(1)} fusion(f32[8,8,128,128]{3,2,1,0:T(8,128)S(1)} %copy-done, f32[64,8,8,128]{3,0,2,1:T(8,128)S(1)} %fusion.64, f32[8,8]{1,0:T(8,128)S(1)} %fusion.91), kind=kOutput, calls=%fused_computation.29 | convolution fusion | flops 805830656 | bytes 6553856 | tf_op jit(solution)/shard_map/ltji,klti->klj/dot_general | solution.py:47
  30.4 8.7 %collective-permute-done.1 = f32[64,1024]{1,0:T(8,128)S(1)} collective-permute-done((f32[64,1024]{1,0:T(8,128)S(1)}, f32[64,1024]{1,0:T(8,128)S(1)}, u32[]{:S(2)}, u32[]{:S(2)}) %collective-permute-start.1) | collective-permute-done | bytes 262176 | tf_op jit(solution)/shard_map/ppermute | solution.py:23
  40.5 7.1 %collective-permute-done.2 = f32[64,1024]{1,0:T(8,128)S(1)} collective-permute-done((f32[64,1024]{1,0:T(8,128)S(1)}, f32[64,1024]{1,0:T(8,128)S(1)}, u32[]{:S(2)}, u32[]{:S(2)}) %collective-permute-start.2) | collective-permute-done | bytes 262176 | tf_op jit(solution)/shard_map/ppermute | solution.py:14
  47.6 6.7 %collective-permute-done.3 = f32[64,1024]{1,0:T(8,128)S(1)} collective-permute-done((f32[64,1024]{1,0:T(8,128)S(1)}, f32[64,1024]{1,0:T(8,128)S(1)}, u32[]{:S(2)}, u32[]{:S(2)}) %collective-permute-start.3) | collective-permute-done | bytes 262176 | tf_op jit(solution)/shard_map/ppermute | solution.py:14
  54.3 6.7 %collective-permute-done.4 = f32[64,1024]{1,0:T(8,128)S(1)} collective-permute-done((f32[64,1024]{1,0:T(8,128)S(1)}, f32[64,1024]{1,0:T(8,128)S(1)}, u32[]{:S(2)}, u32[]{:S(2)}) %collective-permute-start.4) | collective-permute-done | bytes 262176 | tf_op jit(solution)/shard_map/ppermute | solution.py:14
  61.0 6.7 %collective-permute-done.5 = f32[64,1024]{1,0:T(8,128)S(1)} collective-permute-done((f32[64,1024]{1,0:T(8,128)S(1)}, f32[64,1024]{1,0:T(8,128)S(1)}, u32[]{:S(2)}, u32[]{:S(2)}) %collective-permute-start.5) | collective-permute-done | bytes 262176 | tf_op jit(solution)/shard_map/ppermute | solution.py:14
  67.7 6.7 %collective-permute-done.6 = f32[64,1024]{1,0:T(8,128)S(1)} collective-permute-done((f32[64,1024]{1,0:T(8,128)S(1)}, f32[64,1024]{1,0:T(8,128)S(1)}, u32[]{:S(2)}, u32[]{:S(2)}) %collective-permute-start.6) | collective-permute-done | bytes 262176 | tf_op jit(solution)/shard_map/ppermute | solution.py:14
  74.4 6.8 %collective-permute-done.7 = f32[64,1024]{1,0:T(8,128)} collective-permute-done((f32[64,1024]{1,0:T(8,128)S(1)}, f32[64,1024]{1,0:T(8,128)}, u32[]{:S(2)}, u32[]{:S(2)}) %collective-permute-start.7) | collective-permute-done | bytes 262176 | tf_op jit(solution)/shard_map/ppermute | solution.py:14
  102.2 27.1 %reduce-scatter.3.cloned.1.call-done = f32[64,1024]{1,0:T(8,128)} async-done(((f32[64,4096]{1,0:T(8,128)}), f32[64,1024]{1,0:T(8,128)}) %reduce-scatter.3.cloned.1.call-update) | async-done | bytes 262160 | tf_op jit(solution)/shard_map/reduce_scatter | solution.py:80
  129.3 4.9 %fusion.28 = f32[64,1024]{1,0:T(8,128)S(1)} fusion(f32[64,1024]{1,0:T(8,128)} %reduce-scatter.3.cloned.1.call-done, f32[64,1024]{1,0:T(8,128)S(1)} %bitcast_add_fusion.1, f32[1,1024,1024]{2,1,0:T(8,128)} %param.12), kind=kOutput, calls=%fused_computation.31 | convolution fusion | flops 805371904 | bytes 4980736 | tf_op jit(solution)/shard_map/dot_general | solution.py:64
  135.2 39.2 %all-reduce.17 = (f32[64,64]{0,1:T(8,128)S(1)}, f32[64,64]{0,1:T(8,128)S(1)}) all-reduce(f32[64,64]{0,1:T(8,128)S(1)} %fusion.97, f32[64,64]{0,1:T(8,128)S(1)} %fusion.96), channel_id=1, replica_groups=mesh['row'=8,'col'=4] {'row','col'}, use_global_device_ids=true, to_apply=%region_6.9 | all-reduce | flops 8192 | bytes 65536 | tf_op jit(solution)/shard_map/psum | solution.py:98
  174.5 5.8 %cholesky.59 = f32[64,64]{1,0:T(8,128)S(1)} custom-call(f32[64,64]{1,0:T(8,128)S(1)} %fusion.89), custom_call_target="Cholesky" | custom-call | tf_op jit(solution)/shard_map/jit(cholesky)/cholesky | solution.py:85
  182.3 5.7 %custom-call.9 = f32[1,64,64]{1,2,0:T(8,128)S(1)} custom-call(f32[1,64,64]{2,1,0:T(8,128)} %fusion.72), custom_call_target="InvertDiagBlocksLowerTriangular" | custom-call | tf_op jit(solution)/shard_map/jit(_cho_solve)/triangular_solve | solution.py:86
  193.7 4.7 %collective-permute-done.9 = f32[64,1024]{1,0:T(8,128)S(1)} collective-permute-done((f32[64,1024]{1,0:T(8,128)S(1)}, f32[64,1024]{1,0:T(8,128)S(1)}, u32[]{:S(2)}, u32[]{:S(2)}) %collective-permute-start.9) | collective-permute-done | bytes 262176 | tf_op jit(solution)/shard_map/ppermute | solution.py:23
  200.9 4.6 %fusion.25 = f32[64,8,128,1]{2,0,3,1:T(8,128)S(1)} fusion(f32[8,8,128,128]{3,2,1,0:T(8,128)S(1)} %copy-done.1, f32[64,8,8,128]{3,0,2,1:T(8,128)S(1)} %fusion.56, f32[8,8]{1,0:T(8,128)S(1)} %copy-done.18), kind=kOutput, calls=%fused_computation.30 | convolution fusion | flops 805830656 | bytes 6553856 | tf_op jit(solution)/shard_map/ltji,klti->klj/dot_general | solution.py:47
  209.7 9.1 %collective-permute-done.10 = f32[64,1024]{1,0:T(8,128)S(1)} collective-permute-done((f32[64,1024]{1,0:T(8,128)S(1)}, f32[64,1024]{1,0:T(8,128)S(1)}, u32[]{:S(2)}, u32[]{:S(2)}) %collective-permute-start.10) | collective-permute-done | bytes 262176 | tf_op jit(solution)/shard_map/ppermute | solution.py:23
  218.9 6.7 %collective-permute-done.11 = f32[64,1024]{1,0:T(8,128)S(1)} collective-permute-done((f32[64,1024]{1,0:T(8,128)S(1)}, f32[64,1024]{1,0:T(8,128)S(1)}, u32[]{:S(2)}, u32[]{:S(2)}) %collective-permute-start.11) | collective-permute-done | bytes 262176 | tf_op jit(solution)/shard_map/ppermute | solution.py:14
  225.6 6.7 %collective-permute-done.12 = f32[64,1024]{1,0:T(8,128)S(1)} collective-permute-done((f32[64,1024]{1,0:T(8,128)S(1)}, f32[64,1024]{1,0:T(8,128)S(1)}, u32[]{:S(2)}, u32[]{:S(2)}) %collective-permute-start.12) | collective-permute-done | bytes 262176 | tf_op jit(solution)/shard_map/ppermute | solution.py:14
  232.3 6.7 %collective-permute-done.13 = f32[64,1024]{1,0:T(8,128)S(1)} collective-permute-done((f32[64,1024]{1,0:T(8,128)S(1)}, f32[64,1024]{1,0:T(8,128)S(1)}, u32[]{:S(2)}, u32[]{:S(2)}) %collective-permute-start.13) | collective-permute-done | bytes 262176 | tf_op jit(solution)/shard_map/ppermute | solution.py:14
  239.0 6.7 %collective-permute-done.14 = f32[64,1024]{1,0:T(8,128)S(1)} collective-permute-done((f32[64,1024]{1,0:T(8,128)S(1)}, f32[64,1024]{1,0:T(8,128)S(1)}, u32[]{:S(2)}, u32[]{:S(2)}) %collective-permute-start.14) | collective-permute-done | bytes 262176 | tf_op jit(solution)/shard_map/ppermute | solution.py:14
  245.7 6.7 %collective-permute-done.15 = f32[64,1024]{1,0:T(8,128)S(1)} collective-permute-done((f32[64,1024]{1,0:T(8,128)S(1)}, f32[64,1024]{1,0:T(8,128)S(1)}, u32[]{:S(2)}, u32[]{:S(2)}) %collective-permute-start.15) | collective-permute-done | bytes 262176 | tf_op jit(solution)/shard_map/ppermute | solution.py:14
  252.4 6.7 %collective-permute-done.16 = f32[64,1024]{1,0:T(8,128)S(1)} collective-permute-done((f32[64,1024]{1,0:T(8,128)S(1)}, f32[64,1024]{1,0:T(8,128)S(1)}, u32[]{:S(2)}, u32[]{:S(2)}) %collective-permute-start.16) | collective-permute-done | bytes 262176 | tf_op jit(solution)/shard_map/ppermute | solution.py:14
  259.3 6.7 %collective-permute-done.17 = f32[64,1024]{1,0:T(8,128)S(1)} collective-permute-done((f32[64,1024]{1,0:T(8,128)S(1)}, f32[64,1024]{1,0:T(8,128)S(1)}, u32[]{:S(2)}, u32[]{:S(2)}) %collective-permute-start.17) | collective-permute-done | bytes 262176 | tf_op jit(solution)/shard_map/ppermute | solution.py:14
  274.1 5.8 %cholesky.70 = f32[64,64]{1,0:T(8,128)S(1)} custom-call(f32[64,64]{1,0:T(8,128)S(1)} %fusion.84), custom_call_target="Cholesky" | custom-call | tf_op jit(solution)/shard_map/jit(cholesky)/cholesky | solution.py:85
  281.3 4.9 %custom-call.10 = f32[1,64,64]{1,2,0:T(8,128)S(1)} custom-call(f32[1,64,64]{2,1,0:T(8,128)S(1)} %fusion.73), custom_call_target="InvertDiagBlocksLowerTriangular" | custom-call | tf_op jit(solution)/shard_map/jit(_cho_solve)/triangular_solve | solution.py:86
  286.6 15.6 %reduce-scatter.5.cloned.1.call-done = f32[64,1024]{1,0:T(8,128)} async-done(((f32[64,4096]{1,0:T(8,128)}), f32[64,1024]{1,0:T(8,128)}) %reduce-scatter.5.cloned.1.call-update) | async-done | bytes 262160 | tf_op jit(solution)/shard_map/reduce_scatter | solution.py:80
  302.1 4.8 %fusion.31 = f32[64,1024]{1,0:T(8,128)S(1)} fusion(f32[64,1024]{1,0:T(8,128)} %reduce-scatter.5.cloned.1.call-done, f32[64,1024]{1,0:T(8,128)S(1)} %copy-done.3, f32[1,1024,1024]{2,1,0:T(8,128)} %param.12), kind=kOutput, calls=%fused_computation.32 | convolution fusion | flops 805371904 | bytes 4980736 | tf_op jit(solution)/shard_map/dot_general | solution.py:64
  307.7 40.0 %all-reduce.16 = (f32[64,64]{1,0:T(8,128)S(1)}, f32[64,64]{1,0:T(8,128)S(1)}, f32[64,64]{0,1:T(8,128)S(1)}) all-reduce(f32[64,64]{1,0:T(8,128)S(1)} %fusion.100, f32[64,64]{1,0:T(8,128)S(1)} %fusion.99, f32[64,64]{0,1:T(8,128)S(1)} %fusion.98), channel_id=1, replica_groups=mesh['row'=8,'col'=4] {'row','col'}, use_global_device_ids=true, to_apply=%region_10.14 | all-reduce | flops 12288 | bytes 98304 | tf_op jit(solution)/shard_map/psum | solution.py:112
  350.1 5.8 %cholesky.81 = f32[64,64]{1,0:T(8,128)S(1)} custom-call(f32[64,64]{1,0:T(8,128)S(1)} %fusion.79), custom_call_target="Cholesky" | custom-call | tf_op jit(solution)/shard_map/jit(cholesky)/cholesky | solution.py:85
  357.3 4.9 %custom-call.11 = f32[1,64,64]{1,2,0:T(8,128)S(1)} custom-call(f32[1,64,64]{2,1,0:T(8,128)S(1)} %fusion.74), custom_call_target="InvertDiagBlocksLowerTriangular" | custom-call | tf_op jit(solution)/shard_map/jit(_cho_solve)/triangular_solve | solution.py:86
  (169 shorter events, 64.4 us)
Async XLA Ops:
  7.2 122.1 %reduce-scatter.3.cloned.1.call-start = ((), (), s32[]{:S(2)}) async-start(), calls=%async_computation.2 | async-start | bytes 1310720 | tf_op jit(solution)/shard_map/reduce_scatter | solution.py:80
  7.2 10.8 %collective-permute-start = (f32[64,1024]{1,0:T(8,128)}, f32[64,1024]{1,0:T(8,128)S(1)}, u32[]{:S(2)}, u32[]{:S(2)}) collective-permute-start(f32[64,1024]{1,0:T(8,128)} %param.11), channel_id=1, source_target_pairs={{0,1},{1,2},{2,3},{3,4},{4,5},{5,6},{6,7},{7,8},{8,9},{9,10},{10,1... | collective-permute-start | bytes 786440 | tf_op jit(solution)/shard_map/ppermute | solution.py:23
  14.1 12.0 %copy-start.17 = (f32[8,8]{1,0:T(8,128)}, f32[8,8]{1,0:T(8,128)S(1)}, u32[]{:S(2)}) copy-start(f32[8,8]{1,0:T(8,128)S(1)} %fusion.91) | copy-start | bytes 772
  28.7 53.0 %copy-start.8 = (f32[4,1,8,2,12,1024]{5,3,4,2,1,0:T(2,128)S(1)}, f32[4,1,8,2,12,1024]{5,3,4,2,1,0:T(2,128)}, u32[]{:S(2)}) copy-start(f32[4,1,8,2,12,1024]{5,3,4,2,1,0:T(2,128)} %param.13) | copy-start | bytes 9437188
  29.0 10.1 %collective-permute-start.1 = (f32[64,1024]{1,0:T(8,128)S(1)}, f32[64,1024]{1,0:T(8,128)S(1)}, u32[]{:S(2)}, u32[]{:S(2)}) collective-permute-start(f32[64,1024]{1,0:T(8,128)S(1)} %bitcast.318), channel_id=1, source_target_pairs={{1,0},{2,1},{3,2},{4,3},{5,4},{6,5},{7,6},{8,7},{9,8},{10,9},{11,1... | collective-permute-start | bytes 786440 | tf_op jit(solution)/shard_map/ppermute | solution.py:23
  39.2 46.1 %copy-start.19 = (s32[4,1,8]{2,1,0:T(1,128)S(1)}, s32[4,1,8]{2,1,0:T(1,128)}, u32[]{:S(2)}) copy-start(s32[4,1,8]{2,1,0:T(1,128)} %param.14) | copy-start | bytes 388
  39.2 8.4 %collective-permute-start.2 = (f32[64,1024]{1,0:T(8,128)S(1)}, f32[64,1024]{1,0:T(8,128)S(1)}, u32[]{:S(2)}, u32[]{:S(2)}) collective-permute-start(f32[64,1024]{1,0:T(8,128)S(1)} %bitcast_add_fusion.1), channel_id=1, source_target_pairs={{0,4},{4,8},{8,12},{12,16},{16,20},{20,24},{24,28},{28,0},{1,5},{5... | collective-permute-start | bytes 786440 | tf_op jit(solution)/shard_map/ppermute | solution.py:14
  47.6 33.6 %copy-start.9 = (f32[64,1024]{1,0:T(8,128)}, f32[64,1024]{1,0:T(8,128)S(1)}, u32[]{:S(2)}) copy-start(f32[64,1024]{1,0:T(8,128)S(1)} %collective-permute-done.2) | copy-start | bytes 786436
  47.6 6.7 %collective-permute-start.3 = (f32[64,1024]{1,0:T(8,128)S(1)}, f32[64,1024]{1,0:T(8,128)S(1)}, u32[]{:S(2)}, u32[]{:S(2)}) collective-permute-start(f32[64,1024]{1,0:T(8,128)S(1)} %collective-permute-done.2), channel_id=1, source_target_pairs={{0,4},{4,8},{8,12},{12,16},{16,20},{20,24},{24,28},{28,0},{1,5},{5... | collective-permute-start | bytes 786440 | tf_op jit(solution)/shard_map/ppermute | solution.py:14
  54.3 26.9 %copy-start.11 = (f32[64,1024]{1,0:T(8,128)}, f32[64,1024]{1,0:T(8,128)S(1)}, u32[]{:S(2)}) copy-start(f32[64,1024]{1,0:T(8,128)S(1)} %collective-permute-done.3) | copy-start | bytes 786436
  54.3 6.7 %collective-permute-start.4 = (f32[64,1024]{1,0:T(8,128)S(1)}, f32[64,1024]{1,0:T(8,128)S(1)}, u32[]{:S(2)}, u32[]{:S(2)}) collective-permute-start(f32[64,1024]{1,0:T(8,128)S(1)} %collective-permute-done.3), channel_id=1, source_target_pairs={{0,4},{4,8},{8,12},{12,16},{16,20},{20,24},{24,28},{28,0},{1,5},{5... | collective-permute-start | bytes 786440 | tf_op jit(solution)/shard_map/ppermute | solution.py:14
  61.0 20.2 %copy-start.13 = (f32[64,1024]{1,0:T(8,128)}, f32[64,1024]{1,0:T(8,128)S(1)}, u32[]{:S(2)}) copy-start(f32[64,1024]{1,0:T(8,128)S(1)} %collective-permute-done.4) | copy-start | bytes 786436
  61.0 6.7 %collective-permute-start.5 = (f32[64,1024]{1,0:T(8,128)S(1)}, f32[64,1024]{1,0:T(8,128)S(1)}, u32[]{:S(2)}, u32[]{:S(2)}) collective-permute-start(f32[64,1024]{1,0:T(8,128)S(1)} %collective-permute-done.4), channel_id=1, source_target_pairs={{0,4},{4,8},{8,12},{12,16},{16,20},{20,24},{24,28},{28,0},{1,5},{5... | collective-permute-start | bytes 786440 | tf_op jit(solution)/shard_map/ppermute | solution.py:14
  67.7 13.5 %copy-start.15 = (f32[64,1024]{1,0:T(8,128)}, f32[64,1024]{1,0:T(8,128)S(1)}, u32[]{:S(2)}) copy-start(f32[64,1024]{1,0:T(8,128)S(1)} %collective-permute-done.5) | copy-start | bytes 786436
  67.7 6.7 %collective-permute-start.6 = (f32[64,1024]{1,0:T(8,128)S(1)}, f32[64,1024]{1,0:T(8,128)S(1)}, u32[]{:S(2)}, u32[]{:S(2)}) collective-permute-start(f32[64,1024]{1,0:T(8,128)S(1)} %collective-permute-done.5), channel_id=1, source_target_pairs={{0,4},{4,8},{8,12},{12,16},{16,20},{20,24},{24,28},{28,0},{1,5},{5... | collective-permute-start | bytes 786440 | tf_op jit(solution)/shard_map/ppermute | solution.py:14
  74.4 6.8 %collective-permute-start.7 = (f32[64,1024]{1,0:T(8,128)S(1)}, f32[64,1024]{1,0:T(8,128)}, u32[]{:S(2)}, u32[]{:S(2)}) collective-permute-start(f32[64,1024]{1,0:T(8,128)S(1)} %collective-permute-done.6), channel_id=1, source_target_pairs={{0,4},{4,8},{8,12},{12,16},{16,20},{20,24},{24,28},{28,0},{1,5},{5... | collective-permute-start | bytes 786440 | tf_op jit(solution)/shard_map/ppermute | solution.py:14
  81.2 7.6 %collective-permute-start.8 = (f32[64,1024]{1,0:T(8,128)}, f32[64,1024]{1,0:T(8,128)}, u32[]{:S(2)}, u32[]{:S(2)}) collective-permute-start(f32[64,1024]{1,0:T(8,128)} %collective-permute-done.7), channel_id=1, source_target_pairs={{0,4},{4,8},{8,12},{12,16},{16,20},{20,24},{24,28},{28,0},{1,5},{5... | collective-permute-start | bytes 786440 | tf_op jit(solution)/shard_map/ppermute | solution.py:14
  100.6 201.5 %reduce-scatter.5.cloned.1.call-start = ((), (), s32[]{:S(2)}) async-start(), calls=%async_computation.3 | async-start | bytes 1310720 | tf_op jit(solution)/shard_map/reduce_scatter | solution.py:80
  189.9 8.5 %copy-start.6 = (f32[64,1024]{1,0:T(8,128)}, f32[64,1024]{1,0:T(8,128)S(1)}, u32[]{:S(2)}) copy-start(f32[64,1024]{1,0:T(8,128)S(1)} %convolution_subtract_fusion.1) | copy-start | bytes 786436
  189.9 8.5 %collective-permute-start.9 = (f32[64,1024]{1,0:T(8,128)S(1)}, f32[64,1024]{1,0:T(8,128)S(1)}, u32[]{:S(2)}, u32[]{:S(2)}) collective-permute-start(f32[64,1024]{1,0:T(8,128)S(1)} %convolution_subtract_fusion.1), channel_id=1, source_target_pairs={{0,1},{1,2},{2,3},{3,4},{4,5},{5,6},{6,7},{7,8},{8,9},{9,10},{10,1... | collective-permute-start | bytes 786440 | tf_op jit(solution)/shard_map/ppermute | solution.py:23
  208.4 10.4 %collective-permute-start.10 = (f32[64,1024]{1,0:T(8,128)S(1)}, f32[64,1024]{1,0:T(8,128)S(1)}, u32[]{:S(2)}, u32[]{:S(2)}) collective-permute-start(f32[64,1024]{1,0:T(8,128)S(1)} %bitcast.319), channel_id=1, source_target_pairs={{1,0},{2,1},{3,2},{4,3},{5,4},{6,5},{7,6},{8,7},{9,8},{10,9},{11,1... | collective-permute-start | bytes 786440 | tf_op jit(solution)/shard_map/ppermute | solution.py:23
  218.8 47.3 %copy-start.2 = (f32[64,1024]{1,0:T(8,128)}, f32[64,1024]{1,0:T(8,128)S(1)}, u32[]{:S(2)}) copy-start(f32[64,1024]{1,0:T(8,128)S(1)} %bitcast_add_fusion) | copy-start | bytes 786436
  218.8 6.7 %collective-permute-start.11 = (f32[64,1024]{1,0:T(8,128)S(1)}, f32[64,1024]{1,0:T(8,128)S(1)}, u32[]{:S(2)}, u32[]{:S(2)}) collective-permute-start(f32[64,1024]{1,0:T(8,128)S(1)} %bitcast_add_fusion), channel_id=1, source_target_pairs={{0,4},{4,8},{8,12},{12,16},{16,20},{20,24},{24,28},{28,0},{1,5},{5... | collective-permute-start | bytes 786440 | tf_op jit(solution)/shard_map/ppermute | solution.py:14
  225.6 6.7 %collective-permute-start.12 = (f32[64,1024]{1,0:T(8,128)S(1)}, f32[64,1024]{1,0:T(8,128)S(1)}, u32[]{:S(2)}, u32[]{:S(2)}) collective-permute-start(f32[64,1024]{1,0:T(8,128)S(1)} %collective-permute-done.11), channel_id=1, source_target_pairs={{0,4},{4,8},{8,12},{12,16},{16,20},{20,24},{24,28},{28,0},{1,5},{5... | collective-permute-start | bytes 786440 | tf_op jit(solution)/shard_map/ppermute | solution.py:14
  232.3 6.7 %collective-permute-start.13 = (f32[64,1024]{1,0:T(8,128)S(1)}, f32[64,1024]{1,0:T(8,128)S(1)}, u32[]{:S(2)}, u32[]{:S(2)}) collective-permute-start(f32[64,1024]{1,0:T(8,128)S(1)} %collective-permute-done.12), channel_id=1, source_target_pairs={{0,4},{4,8},{8,12},{12,16},{16,20},{20,24},{24,28},{28,0},{1,5},{5... | collective-permute-start | bytes 786440 | tf_op jit(solution)/shard_map/ppermute | solution.py:14
  239.0 6.7 %collective-permute-start.14 = (f32[64,1024]{1,0:T(8,128)S(1)}, f32[64,1024]{1,0:T(8,128)S(1)}, u32[]{:S(2)}, u32[]{:S(2)}) collective-permute-start(f32[64,1024]{1,0:T(8,128)S(1)} %collective-permute-done.13), channel_id=1, source_target_pairs={{0,4},{4,8},{8,12},{12,16},{16,20},{20,24},{24,28},{28,0},{1,5},{5... | collective-permute-start | bytes 786440 | tf_op jit(solution)/shard_map/ppermute | solution.py:14
  245.7 6.7 %collective-permute-start.15 = (f32[64,1024]{1,0:T(8,128)S(1)}, f32[64,1024]{1,0:T(8,128)S(1)}, u32[]{:S(2)}, u32[]{:S(2)}) collective-permute-start(f32[64,1024]{1,0:T(8,128)S(1)} %collective-permute-done.14), channel_id=1, source_target_pairs={{0,4},{4,8},{8,12},{12,16},{16,20},{20,24},{24,28},{28,0},{1,5},{5... | collective-permute-start | bytes 786440 | tf_op jit(solution)/shard_map/ppermute | solution.py:14
  252.4 6.7 %collective-permute-start.16 = (f32[64,1024]{1,0:T(8,128)S(1)}, f32[64,1024]{1,0:T(8,128)S(1)}, u32[]{:S(2)}, u32[]{:S(2)}) collective-permute-start(f32[64,1024]{1,0:T(8,128)S(1)} %collective-permute-done.15), channel_id=1, source_target_pairs={{0,4},{4,8},{8,12},{12,16},{16,20},{20,24},{24,28},{28,0},{1,5},{5... | collective-permute-start | bytes 786440 | tf_op jit(solution)/shard_map/ppermute | solution.py:14
  259.1 6.9 %collective-permute-start.17 = (f32[64,1024]{1,0:T(8,128)S(1)}, f32[64,1024]{1,0:T(8,128)S(1)}, u32[]{:S(2)}, u32[]{:S(2)}) collective-permute-start(f32[64,1024]{1,0:T(8,128)S(1)} %collective-permute-done.16), channel_id=1, source_target_pairs={{0,4},{4,8},{8,12},{12,16},{16,20},{20,24},{24,28},{28,0},{1,5},{5... | collective-permute-start | bytes 786440 | tf_op jit(solution)/shard_map/ppermute | solution.py:14
  273.0 13.2 %copy-start.3 = (f32[64,1024]{1,0:T(8,128)S(1)}, f32[64,1024]{1,0:T(8,128)}, u32[]{:S(2)}) copy-start(f32[64,1024]{1,0:T(8,128)} %copy-done.2) | copy-start | bytes 786436
  273.0 13.2 %copy-start.7 = (f32[64,1024]{1,0:T(8,128)S(1)}, f32[64,1024]{1,0:T(8,128)}, u32[]{:S(2)}) copy-start(f32[64,1024]{1,0:T(8,128)} %copy-done.6) | copy-start | bytes 786436
  286.6 61.6 %copy-start.5 = (f32[64,1024]{1,0:T(8,128)S(1)}, f32[64,1024]{1,0:T(8,128)}, u32[]{:S(2)}) copy-start(f32[64,1024]{1,0:T(8,128)} %copy-done.4) | copy-start | bytes 786436
  (8 other events, 36.0 us)
Sparse Core Ops, SparseCore 0:
  100.8 28.4 reduce-scatter.2
  274.2 27.9 reduce-scatter.4
